TPU v7x, 256 devices: a whole 4x4x8 slice. The times are simulated.
256 devices in a mesh: species: 16 (over y, z_lo, core), tile: 16 (over x, z_hi).
Axes of the slice: x: 4, y: 4, z: 8 (z_hi: 4, z_lo: 2; z = z_hi * 2 + z_lo), core: 2. Of those that a mesh axis runs over, the one named last changes fastest.
Arguments:
- tracers: float32 [256, 16, 128, 128], P('species', None, 'tile'), may hold values from 0.1 to 4
- fluxes: float32 [4, 3, 16, 128, 128], P(None, None, 'species', 'tile'), may hold values from -0.15 to 0.15
- weight_in: bfloat16 [512, 256], replicated, may hold values from -0.375 to 0.375
- weight_out: bfloat16 [256, 512], replicated, may hold values from -0.25 to 0.25
Outputs:
- tracers_out: float32 [256, 16, 128, 128], P('species', None, 'tile')
All inputs are finite; a program needn't handle non-finite values.
Results may differ from a plain program's by a relative error of at most 0.0035.
Values may be sent and summed in bfloat16 or wider, within the bound.
A program may use at most 64 MiB of HBM per device.

v0:
```python
import jax
import jax.numpy as jnp
from jax import lax
from jax.sharding import PartitionSpec as P

STEPS = 4


def extended(cells, sides, width):
    for axis, dim in sides:
        count = lax.axis_size(axis)
        ends = count - 1
        head = lax.slice_in_dim(cells, 0, width, axis=dim)
        tail = lax.slice_in_dim(cells, cells.shape[dim] - width, cells.shape[dim], axis=dim)
        cells = jnp.concatenate(
            [
                lax.ppermute(tail, axis, [(i, (i + 1) % count) for i in range(ends)]),
                cells,
                lax.ppermute(head, axis, [((i + 1) % count, i) for i in range(ends)]),
            ],
            axis=dim,
        )
    return cells


def positive(value):
    return jnp.maximum(value, 0.0)


def negative(value):
    return jnp.minimum(value, 0.0)


def advance(padded_state, padded_x, flux_y, padded_z):
    inner = padded_state[:, 1:-1, 1:-1]
    along_x = padded_state[:, 1:-1]
    face_x = padded_x[:, 1:]
    faces_x = positive(face_x) * along_x[:, :, :-1] + negative(face_x) * along_x[:, :, 1:]
    along_z = padded_state[:, :, 1:-1]
    face_z = padded_z[1:]
    faces_z = positive(face_z) * along_z[:, :-1] + negative(face_z) * along_z[:, 1:]
    faces_y = positive(flux_y) * jnp.roll(inner, 1, 3) + negative(flux_y) * inner
    return (
        inner
        + faces_x[:, :, :-1]
        - faces_x[:, :, 1:]
        + faces_y
        - jnp.roll(faces_y, -1, 3)
        + faces_z[:, :-1]
        - faces_z[:, 1:]
    )


def per_device(tracers, fluxes, weight_in, weight_out):
    spec_loc, depth_all, width_x, width_y = tracers.shape
    tile_at = lax.axis_index("tile")
    grid_shape = (depth_all, width_x, width_y)
    column = tile_at * width_x + lax.broadcasted_iota(jnp.int32, grid_shape, 1)
    level_at = lax.broadcasted_iota(jnp.int32, grid_shape, 0)
    state = tracers
    for interval in range(STEPS):
        gathered = lax.all_gather(fluxes[interval], "species", axis=1, tiled=True)
        flux_x = jnp.where(column == 0, 0.0, gathered[0])
        flux_y = gathered[1]
        flux_z = jnp.where(level_at == 0, 0.0, gathered[2])
        stacked = jnp.concatenate([state, flux_x[None]], 0)
        padded = extended(stacked, (("tile", 2),), 1)
        padded_state = jnp.pad(padded[:spec_loc], ((0, 0), (1, 1), (0, 0), (0, 0)))
        padded_x = padded[spec_loc]
        padded_z = jnp.pad(flux_z, ((1, 1), (0, 0), (0, 0)))
        state = advance(padded_state, padded_x, flux_y, padded_z)
        flattened = state.astype(jnp.bfloat16).reshape(spec_loc, depth_all, width_x * width_y)
        hidden = jax.nn.silu(
            jnp.einsum(
                "hs,szc->hzc",
                weight_in,
                lax.all_to_all(flattened, "species", split_axis=1, concat_axis=0, tiled=True),
                preferred_element_type=jnp.float32,
            )
        ).astype(jnp.bfloat16)
        tendency = (
            0.5 * jnp.einsum("sh,hzc->szc", weight_out, hidden, preferred_element_type=jnp.float32)
        ).astype(jnp.bfloat16)
        returned = lax.all_to_all(tendency, "species", split_axis=0, concat_axis=1, tiled=True)
        state = state + returned.reshape(state.shape).astype(jnp.float32)
    return state


def solution(mesh):
    placed = (P("species", None, "tile", None), P(None, None, "species", "tile", None), P(), P())
    return jax.shard_map(
        per_device,
        mesh=mesh,
        in_specs=placed,
        out_specs=P("species", None, "tile", None),
        check_vma=False,
    )
```

profile of v0, /device:TPU:2, one launch (start us, length us, event | category | flops | bytes accessed | tf_op | source)
XLA Modules:
  0.0 284.3 jit_solution(3213758071041824670)
XLA Ops:
  0.0 0.9 fusion.78
  0.9 21.1 %all-gather = f32[1,3,16,8,128]{4,3,1,0,2:T(8,128)S(1)} all-gather(f32[1,3,1,8,128]{4,3,1,0,2:T(8,128)S(1)} %get-tuple-element.47), channel_id=2, replica_groups=mesh['species'=16,'tile'=16] {'species'}, dimensions={2}, use_global_device_ids=true | all-gather | bytes 208896 | tf_op jit(solution)/shard_map/all_gather | solution.py:62
  21.9 17.0 %all-gather.1 = f32[1,3,16,8,128]{4,3,1,0,2:T(8,128)S(1)} all-gather(f32[1,3,1,8,128]{4,3,1,0,2:T(8,128)S(1)} %get-tuple-element.50), channel_id=3, replica_groups=mesh['species'=16,'tile'=16] {'species'}, dimensions={2}, use_global_device_ids=true | all-gather | bytes 208896 | tf_op jit(solution)/shard_map/all_gather | solution.py:62
  39.0 18.4 %all-gather.2 = f32[1,3,16,8,128]{4,3,1,0,2:T(8,128)S(1)} all-gather(f32[1,3,1,8,128]{4,3,1,0,2:T(8,128)S(1)} %get-tuple-element.49), channel_id=4, replica_groups=mesh['species'=16,'tile'=16] {'species'}, dimensions={2}, use_global_device_ids=true | all-gather | bytes 208896 | tf_op jit(solution)/shard_map/all_gather | solution.py:62
  57.3 17.0 %all-gather.3 = f32[1,3,16,8,128]{4,3,1,0,2:T(8,128)S(1)} all-gather(f32[1,3,1,8,128]{4,3,1,0,2:T(8,128)S(1)} %get-tuple-element.48), channel_id=5, replica_groups=mesh['species'=16,'tile'=16] {'species'}, dimensions={2}, use_global_device_ids=true | all-gather | bytes 208896 | tf_op jit(solution)/shard_map/all_gather | solution.py:62
  74.4 1.6 slice.444
  76.4 0.8 fusion.60
  77.8 7.3 %collective-permute-start.1 = (f32[17,16,1,128]{3,1,2,0:T(8,128)S(1)}, f32[17,16,1,128]{3,1,2,0:T(8,128)S(1)}, u32[]{:S(2)}, u32[]{:S(2)}) collective-permute-start(f32[17,16,1,128]{3,1,2,0:T(8,128)S(1)} %get-tuple-element.20), channel_id=1, source_target_pairs={{1,0},{2,1},{3,2},{4,3},{5,4},{6,5},{7,6},{8,7},{9,8},{10,9},{11,1... | collective-permute-start | bytes 417800 | tf_op jit(solution)/shard_map/ppermute | solution.py:19
  85.1 1.9 collective-permute-start
  87.0 0.7 fusion.53
  87.8 0.7 fusion.62
  88.8 1.5 collective-permute-done.1
  90.3 8.3 %collective-permute-done = f32[17,16,1,128]{3,1,2,0:T(8,128)S(1)} collective-permute-done((f32[17,16,1,128]{3,1,2,0:T(8,128)S(1)}, f32[17,16,1,128]{3,1,2,0:T(8,128)S(1)}, u32[]{:S(2)}, u32[]{:S(2)}) %collective-permute-start) | collective-permute-done | bytes 139296 | tf_op jit(solution)/shard_map/ppermute | solution.py:17
  99.3 0.8 fusion.76
  100.5 13.5 %all_to_all.96 = bf16[16,16,1024]{2,0,1:T(8,128)(2,1)S(1)} all-to-all(bf16[16,16,1024]{2,0,1:T(8,128)(2,1)S(1)} %reshape.116), channel_id=1, replica_groups=mesh['species'=16,'tile'=16] {'species'}, dimensions={1} | all-to-all | bytes 1048576 | tf_op jit(solution)/shard_map/all_to_all | solution.py:77
  114.0 0.9 fusion.28
  115.4 1.1 reduce
  116.7 1.2 reshape.176
  117.9 3.6 %all-to-all-start.1 = ((bf16[16,2,8192]{2,1,0:T(2,128)(2,1)}), bf16[16,2,8192]{2,1,0:T(2,128)(2,1)S(1)}, u32[]{:S(2)}, u32[]{:S(2)}) async-start(bf16[16,2,8192]{2,1,0:T(2,128)(2,1)} %reshape.176), calls=%async_computation.1 | async-start | bytes 1048576 | tf_op jit(solution)/shard_map/all_to_all | solution.py:84
  122.9 9.4 %all-to-all-done.1 = bf16[16,2,8192]{2,1,0:T(2,128)(2,1)S(1)} async-done(((bf16[16,2,8192]{2,1,0:T(2,128)(2,1)}), bf16[16,2,8192]{2,1,0:T(2,128)(2,1)S(1)}, u32[]{:S(2)}, u32[]{:S(2)}) %all-to-all-start.1) | async-done | bytes 524320 | tf_op jit(solution)/shard_map/all_to_all | solution.py:84
  134.1 1.9 collective-permute-start.3
  136.0 4.8 %collective-permute-start.2 = (f32[17,16,1,128]{3,1,2,0:T(8,128)S(1)}, f32[17,16,1,128]{3,1,2,0:T(8,128)S(1)}, u32[]{:S(2)}, u32[]{:S(2)}) collective-permute-start(f32[17,16,1,128]{3,1,2,0:T(8,128)S(1)} %get-tuple-element.17), channel_id=1, source_target_pairs={{0,1},{1,2},{2,3},{3,4},{4,5},{5,6},{6,7},{7,8},{8,9},{9,10},{10,1... | collective-permute-start | bytes 417800 | tf_op jit(solution)/shard_map/ppermute | solution.py:17
  141.6 3.2 %collective-permute-done.3 = f32[17,16,1,128]{3,1,2,0:T(8,128)S(1)} collective-permute-done((f32[17,16,1,128]{3,1,2,0:T(8,128)S(1)}, f32[17,16,1,128]{3,1,2,0:T(8,128)S(1)}, u32[]{:S(2)}, u32[]{:S(2)}) %collective-permute-start.3) | collective-permute-done | bytes 139296 | tf_op jit(solution)/shard_map/ppermute | solution.py:19
  144.7 3.8 %collective-permute-done.2 = f32[17,16,1,128]{3,1,2,0:T(8,128)S(1)} collective-permute-done((f32[17,16,1,128]{3,1,2,0:T(8,128)S(1)}, f32[17,16,1,128]{3,1,2,0:T(8,128)S(1)}, u32[]{:S(2)}, u32[]{:S(2)}) %collective-permute-start.2) | collective-permute-done | bytes 139296 | tf_op jit(solution)/shard_map/ppermute | solution.py:17
  151.0 14.3 %all_to_all.97 = bf16[16,16,1024]{2,0,1:T(8,128)(2,1)S(1)} all-to-all(bf16[16,16,1024]{2,0,1:T(8,128)(2,1)S(1)} %reshape.118), channel_id=1, replica_groups=mesh['species'=16,'tile'=16] {'species'}, dimensions={1} | all-to-all | bytes 1048576 | tf_op jit(solution)/shard_map/all_to_all | solution.py:77
  165.2 0.9 fusion.27
  166.1 1.1 reduce.1
  167.4 1.2 reshape.178
  168.6 3.6 %all-to-all-start.3 = ((bf16[16,2,8192]{2,1,0:T(2,128)(2,1)}), bf16[16,2,8192]{2,1,0:T(2,128)(2,1)S(1)}, u32[]{:S(2)}, u32[]{:S(2)}) async-start(bf16[16,2,8192]{2,1,0:T(2,128)(2,1)} %reshape.178), calls=%async_computation.3 | async-start | bytes 1048576 | tf_op jit(solution)/shard_map/all_to_all | solution.py:84
  173.0 10.0 %all-to-all-done.3 = bf16[16,2,8192]{2,1,0:T(2,128)(2,1)S(1)} async-done(((bf16[16,2,8192]{2,1,0:T(2,128)(2,1)}), bf16[16,2,8192]{2,1,0:T(2,128)(2,1)S(1)}, u32[]{:S(2)}, u32[]{:S(2)}) %all-to-all-start.3) | async-done | bytes 524320 | tf_op jit(solution)/shard_map/all_to_all | solution.py:84
  184.8 1.9 collective-permute-start.5
  186.7 4.8 %collective-permute-start.4 = (f32[17,16,1,128]{3,1,2,0:T(8,128)S(1)}, f32[17,16,1,128]{3,1,2,0:T(8,128)S(1)}, u32[]{:S(2)}, u32[]{:S(2)}) collective-permute-start(f32[17,16,1,128]{3,1,2,0:T(8,128)S(1)} %get-tuple-element.15), channel_id=1, source_target_pairs={{0,1},{1,2},{2,3},{3,4},{4,5},{5,6},{6,7},{7,8},{8,9},{9,10},{10,1... | collective-permute-start | bytes 417800 | tf_op jit(solution)/shard_map/ppermute | solution.py:17
  192.3 1.5 collective-permute-done.5
  193.7 4.3 %collective-permute-done.4 = f32[17,16,1,128]{3,1,2,0:T(8,128)S(1)} collective-permute-done((f32[17,16,1,128]{3,1,2,0:T(8,128)S(1)}, f32[17,16,1,128]{3,1,2,0:T(8,128)S(1)}, u32[]{:S(2)}, u32[]{:S(2)}) %collective-permute-start.4) | collective-permute-done | bytes 139296 | tf_op jit(solution)/shard_map/ppermute | solution.py:17
  199.8 15.5 %all_to_all.98 = bf16[16,16,1024]{2,0,1:T(8,128)(2,1)S(1)} all-to-all(bf16[16,16,1024]{2,0,1:T(8,128)(2,1)S(1)} %reshape.120), channel_id=1, replica_groups=mesh['species'=16,'tile'=16] {'species'}, dimensions={1} | all-to-all | bytes 1048576 | tf_op jit(solution)/shard_map/all_to_all | solution.py:77
  215.4 0.9 fusion.26
  216.3 1.1 reduce.2
  217.6 1.2 reshape.180
  218.7 3.6 %all-to-all-start.5 = ((bf16[16,2,8192]{2,1,0:T(2,128)(2,1)}), bf16[16,2,8192]{2,1,0:T(2,128)(2,1)S(1)}, u32[]{:S(2)}, u32[]{:S(2)}) async-start(bf16[16,2,8192]{2,1,0:T(2,128)(2,1)} %reshape.180), calls=%async_computation.5 | async-start | bytes 1048576 | tf_op jit(solution)/shard_map/all_to_all | solution.py:84
  222.5 10.6 %all-to-all-done.5 = bf16[16,2,8192]{2,1,0:T(2,128)(2,1)S(1)} async-done(((bf16[16,2,8192]{2,1,0:T(2,128)(2,1)}), bf16[16,2,8192]{2,1,0:T(2,128)(2,1)S(1)}, u32[]{:S(2)}, u32[]{:S(2)}) %all-to-all-start.5) | async-done | bytes 524320 | tf_op jit(solution)/shard_map/all_to_all | solution.py:84
  234.9 1.9 collective-permute-start.7
  236.9 5.0 %collective-permute-start.6 = (f32[17,16,1,128]{3,1,2,0:T(8,128)S(1)}, f32[17,16,1,128]{3,1,2,0:T(8,128)S(1)}, u32[]{:S(2)}, u32[]{:S(2)}) collective-permute-start(f32[17,16,1,128]{3,1,2,0:T(8,128)S(1)} %get-tuple-element.13), channel_id=1, source_target_pairs={{0,1},{1,2},{2,3},{3,4},{4,5},{5,6},{6,7},{7,8},{8,9},{9,10},{10,1... | collective-permute-start | bytes 417800 | tf_op jit(solution)/shard_map/ppermute | solution.py:17
  242.9 4.4 %collective-permute-done.6 = f32[17,16,1,128]{3,1,2,0:T(8,128)S(1)} collective-permute-done((f32[17,16,1,128]{3,1,2,0:T(8,128)S(1)}, f32[17,16,1,128]{3,1,2,0:T(8,128)S(1)}, u32[]{:S(2)}, u32[]{:S(2)}) %collective-permute-start.6) | collective-permute-done | bytes 139296 | tf_op jit(solution)/shard_map/ppermute | solution.py:17
  249.1 16.4 %all_to_all.99 = bf16[16,16,1024]{2,0,1:T(8,128)(2,1)S(1)} all-to-all(bf16[16,16,1024]{2,0,1:T(8,128)(2,1)S(1)} %reshape.122), channel_id=1, replica_groups=mesh['species'=16,'tile'=16] {'species'}, dimensions={1} | all-to-all | bytes 1048576 | tf_op jit(solution)/shard_map/all_to_all | solution.py:77
  265.5 0.9 fusion.25
  266.4 1.1 reduce.3
  268.1 13.5 %all_to_all.100 = bf16[16,2,8192]{2,1,0:T(2,128)(2,1)S(1)} all-to-all(bf16[16,2,8192]{2,1,0:T(2,128)(2,1)S(1)} %reshape.182), channel_id=1, replica_groups=mesh['species'=16,'tile'=16] {'species'}, dimensions={0} | all-to-all | bytes 1048576 | tf_op jit(solution)/shard_map/all_to_all | solution.py:84
  283.0 1.3 copy.98
  (132 shorter events, 21.7 us)
Async XLA Ops:
  0.0 114.0 %copy-start = (bf16[256,512]{1,0:T(8,128)(2,1)S(1)}, bf16[256,512]{1,0:T(8,128)(2,1)}, u32[]{:S(2)}) copy-start(bf16[256,512]{1,0:T(8,128)(2,1)} %param.7) | copy-start | bytes 786436
  0.0 75.9 %copy-start.1 = (f32[16,16,8,128]{3,2,1,0:T(8,128)S(1)}, f32[16,16,8,128]{3,2,1,0:T(8,128)}, u32[]{:S(2)}) copy-start(f32[16,16,8,128]{3,2,1,0:T(8,128)} %param.4) | copy-start | bytes 3145732
  77.8 12.5 %collective-permute-start.1 = (f32[17,16,1,128]{3,1,2,0:T(8,128)S(1)}, f32[17,16,1,128]{3,1,2,0:T(8,128)S(1)}, u32[]{:S(2)}, u32[]{:S(2)}) collective-permute-start(f32[17,16,1,128]{3,1,2,0:T(8,128)S(1)} %get-tuple-element.20), channel_id=1, source_target_pairs={{1,0},{2,1},{3,2},{4,3},{5,4},{6,5},{7,6},{8,7},{9,8},{10,9},{11,1... | collective-permute-start | bytes 417800 | tf_op jit(solution)/shard_map/ppermute | solution.py:19
  85.1 13.5 %collective-permute-start = (f32[17,16,1,128]{3,1,2,0:T(8,128)S(1)}, f32[17,16,1,128]{3,1,2,0:T(8,128)S(1)}, u32[]{:S(2)}, u32[]{:S(2)}) collective-permute-start(f32[17,16,1,128]{3,1,2,0:T(8,128)S(1)} %get-tuple-element.19), channel_id=1, source_target_pairs={{0,1},{1,2},{2,3},{3,4},{4,5},{5,6},{6,7},{7,8},{8,9},{9,10},{10,1... | collective-permute-start | bytes 417800 | tf_op jit(solution)/shard_map/ppermute | solution.py:17
  100.1 13.8 %copy-start.13 = (bf16[512,256]{1,0:T(8,128)(2,1)S(1)}, bf16[512,256]{1,0:T(8,128)(2,1)}, u32[]{:S(2)}) copy-start(bf16[512,256]{1,0:T(8,128)(2,1)} %param.6) | copy-start | bytes 786436
  116.7 4.8 %copy-start.12 = (f32[1,16,8,128]{3,2,1,0:T(8,128)S(1)}, f32[1,16,8,128]{3,2,1,0:T(8,128)}, u32[]{:S(2)}) copy-start(f32[1,16,8,128]{3,2,1,0:T(8,128)} %get-tuple-element.56) | copy-start | bytes 196612
  116.7 4.8 %copy-start.7 = (f32[17,8,128]{2,1,0:T(8,128)S(1)}, f32[17,8,128]{2,1,0:T(8,128)}, u32[]{:S(2)}) copy-start(f32[17,8,128]{2,1,0:T(8,128)} %get-tuple-element.59) | copy-start | bytes 208900
  116.7 5.5 %copy-start.6 = (f32[17,8,128]{2,1,0:T(8,128)S(1)}, f32[17,8,128]{2,1,0:T(8,128)}, u32[]{:S(2)}) copy-start(f32[17,8,128]{2,1,0:T(8,128)} %get-tuple-element.60) | copy-start | bytes 208900
  117.9 14.4 %all-to-all-start.1 = ((bf16[16,2,8192]{2,1,0:T(2,128)(2,1)}), bf16[16,2,8192]{2,1,0:T(2,128)(2,1)S(1)}, u32[]{:S(2)}, u32[]{:S(2)}) async-start(bf16[16,2,8192]{2,1,0:T(2,128)(2,1)} %reshape.176), calls=%async_computation.1 | async-start | bytes 1048576 | tf_op jit(solution)/shard_map/all_to_all | solution.py:84
  134.1 10.6 %collective-permute-start.3 = (f32[17,16,1,128]{3,1,2,0:T(8,128)S(1)}, f32[17,16,1,128]{3,1,2,0:T(8,128)S(1)}, u32[]{:S(2)}, u32[]{:S(2)}) collective-permute-start(f32[17,16,1,128]{3,1,2,0:T(8,128)S(1)} %get-tuple-element.18), channel_id=1, source_target_pairs={{1,0},{2,1},{3,2},{4,3},{5,4},{6,5},{7,6},{8,7},{9,8},{10,9},{11,1... | collective-permute-start | bytes 417800 | tf_op jit(solution)/shard_map/ppermute | solution.py:19
  136.0 12.5 %collective-permute-start.2 = (f32[17,16,1,128]{3,1,2,0:T(8,128)S(1)}, f32[17,16,1,128]{3,1,2,0:T(8,128)S(1)}, u32[]{:S(2)}, u32[]{:S(2)}) collective-permute-start(f32[17,16,1,128]{3,1,2,0:T(8,128)S(1)} %get-tuple-element.17), channel_id=1, source_target_pairs={{0,1},{1,2},{2,3},{3,4},{4,5},{5,6},{6,7},{7,8},{8,9},{9,10},{10,1... | collective-permute-start | bytes 417800 | tf_op jit(solution)/shard_map/ppermute | solution.py:17
  148.5 0.9 copy-start.2
  148.6 0.9 copy-start.3
  150.6 14.7 %copy-start.14 = (bf16[512,256]{1,0:T(8,128)(2,1)S(1)}, bf16[512,256]{1,0:T(8,128)(2,1)}, u32[]{:S(2)}) copy-start(bf16[512,256]{1,0:T(8,128)(2,1)} %param.6) | copy-start | bytes 786436
  167.2 5.0 %copy-start.11 = (f32[1,16,8,128]{3,2,1,0:T(8,128)S(1)}, f32[1,16,8,128]{3,2,1,0:T(8,128)}, u32[]{:S(2)}) copy-start(f32[1,16,8,128]{3,2,1,0:T(8,128)} %get-tuple-element.57) | copy-start | bytes 196612
  167.2 5.0 %copy-start.8 = (f32[16,8,128]{2,1,0:T(8,128)S(1)}, f32[16,8,128]{2,1,0:T(8,128)}, u32[]{:S(2)}) copy-start(f32[16,8,128]{2,1,0:T(8,128)} %get-tuple-element.51) | copy-start | bytes 196612
  167.2 5.0 %copy-start.9 = (f32[16,8,128]{2,1,0:T(8,128)S(1)}, f32[16,8,128]{2,1,0:T(8,128)}, u32[]{:S(2)}) copy-start(f32[16,8,128]{2,1,0:T(8,128)} %get-tuple-element.53) | copy-start | bytes 196612
  168.6 14.4 %all-to-all-start.3 = ((bf16[16,2,8192]{2,1,0:T(2,128)(2,1)}), bf16[16,2,8192]{2,1,0:T(2,128)(2,1)S(1)}, u32[]{:S(2)}, u32[]{:S(2)}) async-start(bf16[16,2,8192]{2,1,0:T(2,128)(2,1)} %reshape.178), calls=%async_computation.3 | async-start | bytes 1048576 | tf_op jit(solution)/shard_map/all_to_all | solution.py:84
  184.8 9.0 %collective-permute-start.5 = (f32[17,16,1,128]{3,1,2,0:T(8,128)S(1)}, f32[17,16,1,128]{3,1,2,0:T(8,128)S(1)}, u32[]{:S(2)}, u32[]{:S(2)}) collective-permute-start(f32[17,16,1,128]{3,1,2,0:T(8,128)S(1)} %get-tuple-element.16), channel_id=1, source_target_pairs={{1,0},{2,1},{3,2},{4,3},{5,4},{6,5},{7,6},{8,7},{9,8},{10,9},{11,1... | collective-permute-start | bytes 417800 | tf_op jit(solution)/shard_map/ppermute | solution.py:19
  186.7 11.3 %collective-permute-start.4 = (f32[17,16,1,128]{3,1,2,0:T(8,128)S(1)}, f32[17,16,1,128]{3,1,2,0:T(8,128)S(1)}, u32[]{:S(2)}, u32[]{:S(2)}) collective-permute-start(f32[17,16,1,128]{3,1,2,0:T(8,128)S(1)} %get-tuple-element.15), channel_id=1, source_target_pairs={{0,1},{1,2},{2,3},{3,4},{4,5},{5,6},{6,7},{7,8},{8,9},{9,10},{10,1... | collective-permute-start | bytes 417800 | tf_op jit(solution)/shard_map/ppermute | solution.py:17
  199.4 15.9 %copy-start.15 = (bf16[512,256]{1,0:T(8,128)(2,1)S(1)}, bf16[512,256]{1,0:T(8,128)(2,1)}, u32[]{:S(2)}) copy-start(bf16[512,256]{1,0:T(8,128)(2,1)} %param.6) | copy-start | bytes 786436
  217.3 5.0 %copy-start.10 = (f32[1,16,8,128]{3,2,1,0:T(8,128)S(1)}, f32[1,16,8,128]{3,2,1,0:T(8,128)}, u32[]{:S(2)}) copy-start(f32[1,16,8,128]{3,2,1,0:T(8,128)} %get-tuple-element.58) | copy-start | bytes 196612
  217.3 5.0 %copy-start.5 = (f32[17,8,128]{2,1,0:T(8,128)S(1)}, f32[17,8,128]{2,1,0:T(8,128)}, u32[]{:S(2)}) copy-start(f32[17,8,128]{2,1,0:T(8,128)} %get-tuple-element.61) | copy-start | bytes 208900
  217.3 5.0 %copy-start.4 = (f32[17,8,128]{2,1,0:T(8,128)S(1)}, f32[17,8,128]{2,1,0:T(8,128)}, u32[]{:S(2)}) copy-start(f32[17,8,128]{2,1,0:T(8,128)} %get-tuple-element.62) | copy-start | bytes 208900
  218.7 14.4 %all-to-all-start.5 = ((bf16[16,2,8192]{2,1,0:T(2,128)(2,1)}), bf16[16,2,8192]{2,1,0:T(2,128)(2,1)S(1)}, u32[]{:S(2)}, u32[]{:S(2)}) async-start(bf16[16,2,8192]{2,1,0:T(2,128)(2,1)} %reshape.180), calls=%async_computation.5 | async-start | bytes 1048576 | tf_op jit(solution)/shard_map/all_to_all | solution.py:84
  234.9 8.0 %collective-permute-start.7 = (f32[17,16,1,128]{3,1,2,0:T(8,128)S(1)}, f32[17,16,1,128]{3,1,2,0:T(8,128)S(1)}, u32[]{:S(2)}, u32[]{:S(2)}) collective-permute-start(f32[17,16,1,128]{3,1,2,0:T(8,128)S(1)} %get-tuple-element.14), channel_id=1, source_target_pairs={{1,0},{2,1},{3,2},{4,3},{5,4},{6,5},{7,6},{8,7},{9,8},{10,9},{11,1... | collective-permute-start | bytes 417800 | tf_op jit(solution)/shard_map/ppermute | solution.py:19
  236.9 10.4 %collective-permute-start.6 = (f32[17,16,1,128]{3,1,2,0:T(8,128)S(1)}, f32[17,16,1,128]{3,1,2,0:T(8,128)S(1)}, u32[]{:S(2)}, u32[]{:S(2)}) collective-permute-start(f32[17,16,1,128]{3,1,2,0:T(8,128)S(1)} %get-tuple-element.13), channel_id=1, source_target_pairs={{0,1},{1,2},{2,3},{3,4},{4,5},{5,6},{6,7},{7,8},{8,9},{9,10},{10,1... | collective-permute-start | bytes 417800 | tf_op jit(solution)/shard_map/ppermute | solution.py:17
  248.7 16.8 %copy-start.16 = (bf16[512,256]{1,0:T(8,128)(2,1)S(1)}, bf16[512,256]{1,0:T(8,128)(2,1)}, u32[]{:S(2)}) copy-start(bf16[512,256]{1,0:T(8,128)(2,1)} %param.6) | copy-start | bytes 786436
where the time goes:
time: 285 us; the launch traced here: 284 us
  blocking collectives  147 us (52%)
  waiting for transfers between devices  57.1 us (20%)
  starting transfers between devices  40.4 us (14%)
  local copies, waits for them, and re-layouts  18.7 us (7%)
  other arithmetic  17.2 us (6%)
  matrix products  3.48 us (1%)
    all_gather x4, blocking collectives, per_device(): gathered = lax.all_gather(fluxes[interval], 'species', axis=1, tiled=True)  73.5 us
    all_to_all x4, blocking collectives, per_device(): lax.all_to_all(flattened, 'species', split_axis=1, concat_axis=0, tiled=T...  59.7 us
    all_to_all x3, waiting for transfers between devices, per_device(): lax.all_to_all(tendency, 'species', split_axis=0, concat_axis=1, tiled=True)  30 us
    ppermute x4, waiting for transfers between devices, extended(): lax.ppermute(tail, axis, [(i, (i + 1) % count) for i in range(ends)])  20.7 us
    ppermute x4, starting transfers between devices, extended(): lax.ppermute(tail, axis, [(i, (i + 1) % count) for i in range(ends)])  16.6 us
    all_to_all x1, blocking collectives, per_device(): lax.all_to_all(tendency, 'species', split_axis=0, concat_axis=1, tiled=True)  13.5 us
    ppermute x4, starting transfers between devices, extended(): lax.ppermute(head, axis, [((i + 1) % count, i) for i in range(ends)])  13 us
    all_to_all x3, starting transfers between devices, per_device(): lax.all_to_all(tendency, 'species', split_axis=0, concat_axis=1, tiled=True)  10.7 us
  transfers between devices with their start and end apart: 11, of which 11 were waited for; matrix products, arithmetic and copies ran while one was open for 2% of the time, Pallas kernels for 0%

commit v1 on v0

--- a/solution.py
+++ b/solution.py
@@ -59,7 +59,12 @@
     level_at = lax.broadcasted_iota(jnp.int32, grid_shape, 0)
     state = tracers
     for interval in range(STEPS):
-        gathered = lax.all_gather(fluxes[interval], "species", axis=1, tiled=True)
+        gathered = jnp.concatenate(
+            lax.all_to_all(
+                jnp.stack([fluxes[interval]] * lax.axis_size("species")), "species", 0, 0
+            ),
+            axis=1,
+        )
         flux_x = jnp.where(column == 0, 0.0, gathered[0])
         flux_y = gathered[1]
         flux_z = jnp.where(level_at == 0, 0.0, gathered[2])

time: 285 us -> 257 us (0.902)
  blocking collectives: 147 us -> 109 us
  starting transfers between devices: 40.4 us -> 44.5 us
    all_gather x4 -> x0, blocking collectives: 73.5 us -> none  [per_device(): gathered = lax.all_gather(fluxes[interval], 'species', axis=1, tiled=True)]
    all_to_all x0 -> x3, blocking collectives: none -> 34.4 us  [per_device(): lax.all_to_all(jnp.stack([fluxes[interval]] * lax.axis_size('species')),...]
    all_to_all x0 -> x1, starting transfers between devices: none -> 4.18 us  [per_device(): lax.all_to_all(jnp.stack([fluxes[interval]] * lax.axis_size('species')),...]
    all_to_all x0 -> x3, local copies, waits for them, and re-layouts: none -> 4.17 us  [per_device(): lax.all_to_all(jnp.stack([fluxes[interval]] * lax.axis_size('species')),...]
    unnamed x52 -> x36, local copies, waits for them, and re-layouts: 8.29 us -> 7.65 us
  transfers between devices with their start and end apart: 11 -> 12, of which waited for: 11 -> 12; matrix products, arithmetic and copies ran while one was open for 2% -> 4% of each run, Pallas kernels for 0% -> 0%
where the time goes in v1:
time: 257 us; the launch traced here: 255 us
  blocking collectives  109 us (42%)
  waiting for transfers between devices  57.5 us (22%)
  starting transfers between devices  44.5 us (17%)
  local copies, waits for them, and re-layouts  20.4 us (8%)
  other arithmetic  20 us (8%)
  matrix products  3.49 us (1%)
    all_to_all x4, blocking collectives, per_device(): lax.all_to_all(flattened, 'species', split_axis=1, concat_axis=0, tiled=T...  60.7 us
    all_to_all x3, blocking collectives, per_device(): lax.all_to_all(jnp.stack([fluxes[interval]] * lax.axis_size('species')),...  34.4 us
    all_to_all x3, waiting for transfers between devices, per_device(): lax.all_to_all(tendency, 'species', split_axis=0, concat_axis=1, tiled=True)  29.4 us
    ppermute x4, waiting for transfers between devices, extended(): lax.ppermute(tail, axis, [(i, (i + 1) % count) for i in range(ends)])  19.8 us
    ppermute x4, starting transfers between devices, extended(): lax.ppermute(tail, axis, [(i, (i + 1) % count) for i in range(ends)])  16.5 us
    all_to_all x1, blocking collectives, per_device(): lax.all_to_all(tendency, 'species', split_axis=0, concat_axis=1, tiled=True)  13.5 us
    ppermute x4, starting transfers between devices, extended(): lax.ppermute(head, axis, [((i + 1) % count, i) for i in range(ends)])  13.2 us
    all_to_all x3, starting transfers between devices, per_device(): lax.all_to_all(tendency, 'species', split_axis=0, concat_axis=1, tiled=True)  10.7 us
  transfers between devices with their start and end apart: 12, of which 12 were waited for; matrix products, arithmetic and copies ran while one was open for 4% of the time, Pallas kernels for 0%

profile of v1, /device:TPU:2, one launch (start us, length us, event | category | flops | bytes accessed | tf_op | source)
XLA Modules:
  0.0 255.3 jit_solution(14831959644512778129)
XLA Ops:
  0.9 13.2 %all_to_all.116 = f32[16,3,1,8,128]{4,3,2,1,0:T(8,128)} all-to-all(f32[16,3,1,8,128]{4,3,2,1,0:T(8,128)S(1)} %stack.12), channel_id=1, replica_groups=mesh['species'=16,'tile'=16] {'species'}, dimensions={0} | all-to-all | bytes 393216 | tf_op jit(solution)/shard_map/all_to_all | solution.py:63
  14.1 10.6 %all_to_all.117 = f32[16,3,1,8,128]{4,3,2,1,0:T(8,128)} all-to-all(f32[16,3,1,8,128]{4,3,2,1,0:T(8,128)S(1)} %stack.13), channel_id=1, replica_groups=mesh['species'=16,'tile'=16] {'species'}, dimensions={0} | all-to-all | bytes 393216 | tf_op jit(solution)/shard_map/all_to_all | solution.py:63
  24.7 10.6 %all_to_all.118 = f32[16,3,1,8,128]{4,3,2,1,0:T(8,128)} all-to-all(f32[16,3,1,8,128]{4,3,2,1,0:T(8,128)S(1)} %stack.14), channel_id=1, replica_groups=mesh['species'=16,'tile'=16] {'species'}, dimensions={0} | all-to-all | bytes 393216 | tf_op jit(solution)/shard_map/all_to_all | solution.py:63
  36.0 4.2 %all-to-all-start.9 = ((f32[16,3,1,8,128]{4,3,2,1,0:T(8,128)}), f32[16,3,1,8,128]{4,3,2,1,0:T(8,128)}, u32[]{:S(2)}, u32[]{:S(2)}) async-start(f32[16,3,1,8,128]{4,3,2,1,0:T(8,128)} %stack.15), calls=%async_computation.9 | async-start | bytes 393216 | tf_op jit(solution)/shard_map/all_to_all | solution.py:63
  41.8 1.6 copy.94
  43.4 1.6 copy.93
  45.1 2.4 all-to-all-done.9
  47.5 0.9 copy.92
  48.5 1.7 fusion.60
  50.9 7.3 %collective-permute-start.1 = (f32[17,16,1,128]{3,1,2,0:T(8,128)S(1)}, f32[17,16,1,128]{3,1,2,0:T(8,128)S(1)}, u32[]{:S(2)}, u32[]{:S(2)}) collective-permute-start(f32[17,16,1,128]{3,1,2,0:T(8,128)S(1)} %get-tuple-element.20), channel_id=1, source_target_pairs={{1,0},{2,1},{3,2},{4,3},{5,4},{6,5},{7,6},{8,7},{9,8},{10,9},{11,1... | collective-permute-start | bytes 417800 | tf_op jit(solution)/shard_map/ppermute | solution.py:19
  58.1 1.9 collective-permute-start
  60.1 1.0 fusion.53
  61.5 1.1 collective-permute-done.1
  62.6 7.6 %collective-permute-done = f32[17,16,1,128]{3,1,2,0:T(8,128)S(1)} collective-permute-done((f32[17,16,1,128]{3,1,2,0:T(8,128)S(1)}, f32[17,16,1,128]{3,1,2,0:T(8,128)S(1)}, u32[]{:S(2)}, u32[]{:S(2)}) %collective-permute-start) | collective-permute-done | bytes 139296 | tf_op jit(solution)/shard_map/ppermute | solution.py:17
  72.1 14.1 %all_to_all.119 = bf16[16,16,1024]{2,0,1:T(8,128)(2,1)S(1)} all-to-all(bf16[16,16,1024]{2,0,1:T(8,128)(2,1)S(1)} %reshape.265), channel_id=1, replica_groups=mesh['species'=16,'tile'=16] {'species'}, dimensions={1} | all-to-all | bytes 1048576 | tf_op jit(solution)/shard_map/all_to_all | solution.py:82
  86.2 0.9 fusion.28
  87.6 0.9 reduce
  88.8 1.2 reshape.284
  90.0 3.6 %all-to-all-start.2 = ((bf16[16,2,8192]{2,1,0:T(2,128)(2,1)}), bf16[16,2,8192]{2,1,0:T(2,128)(2,1)S(1)}, u32[]{:S(2)}, u32[]{:S(2)}) async-start(bf16[16,2,8192]{2,1,0:T(2,128)(2,1)} %reshape.284), calls=%async_computation.2 | async-start | bytes 1048576 | tf_op jit(solution)/shard_map/all_to_all | solution.py:89
  94.5 9.8 %all-to-all-done.2 = bf16[16,2,8192]{2,1,0:T(2,128)(2,1)S(1)} async-done(((bf16[16,2,8192]{2,1,0:T(2,128)(2,1)}), bf16[16,2,8192]{2,1,0:T(2,128)(2,1)S(1)}, u32[]{:S(2)}, u32[]{:S(2)}) %all-to-all-start.2) | async-done | bytes 524320 | tf_op jit(solution)/shard_map/all_to_all | solution.py:89
  106.2 2.1 collective-permute-start.3
  108.2 4.7 %collective-permute-start.2 = (f32[17,16,1,128]{3,1,2,0:T(8,128)S(1)}, f32[17,16,1,128]{3,1,2,0:T(8,128)S(1)}, u32[]{:S(2)}, u32[]{:S(2)}) collective-permute-start(f32[17,16,1,128]{3,1,2,0:T(8,128)S(1)} %get-tuple-element.17), channel_id=1, source_target_pairs={{0,1},{1,2},{2,3},{3,4},{4,5},{5,6},{6,7},{7,8},{8,9},{9,10},{10,1... | collective-permute-start | bytes 417800 | tf_op jit(solution)/shard_map/ppermute | solution.py:17
  113.7 3.2 %collective-permute-done.3 = f32[17,16,1,128]{3,1,2,0:T(8,128)S(1)} collective-permute-done((f32[17,16,1,128]{3,1,2,0:T(8,128)S(1)}, f32[17,16,1,128]{3,1,2,0:T(8,128)S(1)}, u32[]{:S(2)}, u32[]{:S(2)}) %collective-permute-start.3) | collective-permute-done | bytes 139296 | tf_op jit(solution)/shard_map/ppermute | solution.py:19
  116.9 3.7 %collective-permute-done.2 = f32[17,16,1,128]{3,1,2,0:T(8,128)S(1)} collective-permute-done((f32[17,16,1,128]{3,1,2,0:T(8,128)S(1)}, f32[17,16,1,128]{3,1,2,0:T(8,128)S(1)}, u32[]{:S(2)}, u32[]{:S(2)}) %collective-permute-start.2) | collective-permute-done | bytes 139296 | tf_op jit(solution)/shard_map/ppermute | solution.py:17
  122.4 14.3 %all_to_all.120 = bf16[16,16,1024]{2,0,1:T(8,128)(2,1)S(1)} all-to-all(bf16[16,16,1024]{2,0,1:T(8,128)(2,1)S(1)} %reshape.268), channel_id=1, replica_groups=mesh['species'=16,'tile'=16] {'species'}, dimensions={1} | all-to-all | bytes 1048576 | tf_op jit(solution)/shard_map/all_to_all | solution.py:82
  136.7 0.9 fusion.27
  137.5 0.9 reduce.1
  138.7 1.2 reshape.286
  139.9 3.6 %all-to-all-start.5 = ((bf16[16,2,8192]{2,1,0:T(2,128)(2,1)}), bf16[16,2,8192]{2,1,0:T(2,128)(2,1)S(1)}, u32[]{:S(2)}, u32[]{:S(2)}) async-start(bf16[16,2,8192]{2,1,0:T(2,128)(2,1)} %reshape.286), calls=%async_computation.5 | async-start | bytes 1048576 | tf_op jit(solution)/shard_map/all_to_all | solution.py:89
  144.5 9.8 %all-to-all-done.5 = bf16[16,2,8192]{2,1,0:T(2,128)(2,1)S(1)} async-done(((bf16[16,2,8192]{2,1,0:T(2,128)(2,1)}), bf16[16,2,8192]{2,1,0:T(2,128)(2,1)S(1)}, u32[]{:S(2)}, u32[]{:S(2)}) %all-to-all-start.5) | async-done | bytes 524320 | tf_op jit(solution)/shard_map/all_to_all | solution.py:89
  156.1 1.9 collective-permute-start.5
  158.0 4.8 %collective-permute-start.4 = (f32[17,16,1,128]{3,1,2,0:T(8,128)S(1)}, f32[17,16,1,128]{3,1,2,0:T(8,128)S(1)}, u32[]{:S(2)}, u32[]{:S(2)}) collective-permute-start(f32[17,16,1,128]{3,1,2,0:T(8,128)S(1)} %get-tuple-element.15), channel_id=1, source_target_pairs={{0,1},{1,2},{2,3},{3,4},{4,5},{5,6},{6,7},{7,8},{8,9},{9,10},{10,1... | collective-permute-start | bytes 417800 | tf_op jit(solution)/shard_map/ppermute | solution.py:17
  163.6 1.3 collective-permute-done.5
  164.9 4.5 %collective-permute-done.4 = f32[17,16,1,128]{3,1,2,0:T(8,128)S(1)} collective-permute-done((f32[17,16,1,128]{3,1,2,0:T(8,128)S(1)}, f32[17,16,1,128]{3,1,2,0:T(8,128)S(1)}, u32[]{:S(2)}, u32[]{:S(2)}) %collective-permute-start.4) | collective-permute-done | bytes 139296 | tf_op jit(solution)/shard_map/ppermute | solution.py:17
  171.1 15.5 %all_to_all.121 = bf16[16,16,1024]{2,0,1:T(8,128)(2,1)S(1)} all-to-all(bf16[16,16,1024]{2,0,1:T(8,128)(2,1)S(1)} %reshape.271), channel_id=1, replica_groups=mesh['species'=16,'tile'=16] {'species'}, dimensions={1} | all-to-all | bytes 1048576 | tf_op jit(solution)/shard_map/all_to_all | solution.py:82
  186.7 0.9 fusion.26
  187.6 0.9 reduce.2
  188.7 1.2 reshape.288
  189.9 3.6 %all-to-all-start.8 = ((bf16[16,2,8192]{2,1,0:T(2,128)(2,1)}), bf16[16,2,8192]{2,1,0:T(2,128)(2,1)S(1)}, u32[]{:S(2)}, u32[]{:S(2)}) async-start(bf16[16,2,8192]{2,1,0:T(2,128)(2,1)} %reshape.288), calls=%async_computation.8 | async-start | bytes 1048576 | tf_op jit(solution)/shard_map/all_to_all | solution.py:89
  194.5 9.8 %all-to-all-done.8 = bf16[16,2,8192]{2,1,0:T(2,128)(2,1)S(1)} async-done(((bf16[16,2,8192]{2,1,0:T(2,128)(2,1)}), bf16[16,2,8192]{2,1,0:T(2,128)(2,1)S(1)}, u32[]{:S(2)}, u32[]{:S(2)}) %all-to-all-start.8) | async-done | bytes 524320 | tf_op jit(solution)/shard_map/all_to_all | solution.py:89
  206.1 1.9 collective-permute-start.7
  208.0 5.0 %collective-permute-start.6 = (f32[17,16,1,128]{3,1,2,0:T(8,128)S(1)}, f32[17,16,1,128]{3,1,2,0:T(8,128)S(1)}, u32[]{:S(2)}, u32[]{:S(2)}) collective-permute-start(f32[17,16,1,128]{3,1,2,0:T(8,128)S(1)} %get-tuple-element.13), channel_id=1, source_target_pairs={{0,1},{1,2},{2,3},{3,4},{4,5},{5,6},{6,7},{7,8},{8,9},{9,10},{10,1... | collective-permute-start | bytes 417800 | tf_op jit(solution)/shard_map/ppermute | solution.py:17
  214.1 4.0 %collective-permute-done.6 = f32[17,16,1,128]{3,1,2,0:T(8,128)S(1)} collective-permute-done((f32[17,16,1,128]{3,1,2,0:T(8,128)S(1)}, f32[17,16,1,128]{3,1,2,0:T(8,128)S(1)}, u32[]{:S(2)}, u32[]{:S(2)}) %collective-permute-start.6) | collective-permute-done | bytes 139296 | tf_op jit(solution)/shard_map/ppermute | solution.py:17
  219.9 16.8 %all_to_all.122 = bf16[16,16,1024]{2,0,1:T(8,128)(2,1)S(1)} all-to-all(bf16[16,16,1024]{2,0,1:T(8,128)(2,1)S(1)} %reshape.274), channel_id=1, replica_groups=mesh['species'=16,'tile'=16] {'species'}, dimensions={1} | all-to-all | bytes 1048576 | tf_op jit(solution)/shard_map/all_to_all | solution.py:82
  236.7 0.9 fusion.25
  237.6 0.9 reduce.3
  239.1 13.5 %all_to_all.123 = bf16[16,2,8192]{2,1,0:T(2,128)(2,1)S(1)} all-to-all(bf16[16,2,8192]{2,1,0:T(2,128)(2,1)S(1)} %reshape.290), channel_id=1, replica_groups=mesh['species'=16,'tile'=16] {'species'}, dimensions={0} | all-to-all | bytes 1048576 | tf_op jit(solution)/shard_map/all_to_all | solution.py:89
  254.0 1.3 copy.67
  (124 shorter events, 25.2 us)
Async XLA Ops:
  0.0 86.2 %copy-start = (bf16[256,512]{1,0:T(8,128)(2,1)S(1)}, bf16[256,512]{1,0:T(8,128)(2,1)}, u32[]{:S(2)}) copy-start(bf16[256,512]{1,0:T(8,128)(2,1)} %param.7) | copy-start | bytes 786436
  0.0 40.2 %copy-start.1 = (f32[16,16,8,128]{3,2,1,0:T(8,128)S(1)}, f32[16,16,8,128]{3,2,1,0:T(8,128)}, u32[]{:S(2)}) copy-start(f32[16,16,8,128]{3,2,1,0:T(8,128)} %param.4) | copy-start | bytes 3145732
  36.0 11.5 %all-to-all-start.9 = ((f32[16,3,1,8,128]{4,3,2,1,0:T(8,128)}), f32[16,3,1,8,128]{4,3,2,1,0:T(8,128)}, u32[]{:S(2)}, u32[]{:S(2)}) async-start(f32[16,3,1,8,128]{4,3,2,1,0:T(8,128)} %stack.15), calls=%async_computation.9 | async-start | bytes 393216 | tf_op jit(solution)/shard_map/all_to_all | solution.py:63
  48.4 11.6 %copy-start.2 = (f32[16,3,1,8,128]{4,3,0,2,1:T(8,128)}, f32[16,3,1,8,128]{4,3,0,2,1:T(8,128)S(1)}, u32[]{:S(2)}) copy-start(f32[16,3,1,8,128]{4,3,0,2,1:T(8,128)S(1)} %copy.92) | copy-start | bytes 589828
  50.9 11.7 %collective-permute-start.1 = (f32[17,16,1,128]{3,1,2,0:T(8,128)S(1)}, f32[17,16,1,128]{3,1,2,0:T(8,128)S(1)}, u32[]{:S(2)}, u32[]{:S(2)}) collective-permute-start(f32[17,16,1,128]{3,1,2,0:T(8,128)S(1)} %get-tuple-element.20), channel_id=1, source_target_pairs={{1,0},{2,1},{3,2},{4,3},{5,4},{6,5},{7,6},{8,7},{9,8},{10,9},{11,1... | collective-permute-start | bytes 417800 | tf_op jit(solution)/shard_map/ppermute | solution.py:19
  58.1 12.1 %collective-permute-start = (f32[17,16,1,128]{3,1,2,0:T(8,128)S(1)}, f32[17,16,1,128]{3,1,2,0:T(8,128)S(1)}, u32[]{:S(2)}, u32[]{:S(2)}) collective-permute-start(f32[17,16,1,128]{3,1,2,0:T(8,128)S(1)} %get-tuple-element.19), channel_id=1, source_target_pairs={{0,1},{1,2},{2,3},{3,4},{4,5},{5,6},{6,7},{7,8},{8,9},{9,10},{10,1... | collective-permute-start | bytes 417800 | tf_op jit(solution)/shard_map/ppermute | solution.py:17
  71.7 14.5 %copy-start.6 = (bf16[512,256]{1,0:T(8,128)(2,1)S(1)}, bf16[512,256]{1,0:T(8,128)(2,1)}, u32[]{:S(2)}) copy-start(bf16[512,256]{1,0:T(8,128)(2,1)} %param.6) | copy-start | bytes 786436
  88.6 5.0 %copy-start.5 = (f32[1,16,8,128]{3,2,1,0:T(8,128)S(1)}, f32[1,16,8,128]{3,2,1,0:T(8,128)}, u32[]{:S(2)}) copy-start(f32[1,16,8,128]{3,2,1,0:T(8,128)} %get-tuple-element.56) | copy-start | bytes 196612
  90.0 14.4 %all-to-all-start.2 = ((bf16[16,2,8192]{2,1,0:T(2,128)(2,1)}), bf16[16,2,8192]{2,1,0:T(2,128)(2,1)S(1)}, u32[]{:S(2)}, u32[]{:S(2)}) async-start(bf16[16,2,8192]{2,1,0:T(2,128)(2,1)} %reshape.284), calls=%async_computation.2 | async-start | bytes 1048576 | tf_op jit(solution)/shard_map/all_to_all | solution.py:89
  106.2 10.7 %collective-permute-start.3 = (f32[17,16,1,128]{3,1,2,0:T(8,128)S(1)}, f32[17,16,1,128]{3,1,2,0:T(8,128)S(1)}, u32[]{:S(2)}, u32[]{:S(2)}) collective-permute-start(f32[17,16,1,128]{3,1,2,0:T(8,128)S(1)} %get-tuple-element.18), channel_id=1, source_target_pairs={{1,0},{2,1},{3,2},{4,3},{5,4},{6,5},{7,6},{8,7},{9,8},{10,9},{11,1... | collective-permute-start | bytes 417800 | tf_op jit(solution)/shard_map/ppermute | solution.py:19
  108.2 12.4 %collective-permute-start.2 = (f32[17,16,1,128]{3,1,2,0:T(8,128)S(1)}, f32[17,16,1,128]{3,1,2,0:T(8,128)S(1)}, u32[]{:S(2)}, u32[]{:S(2)}) collective-permute-start(f32[17,16,1,128]{3,1,2,0:T(8,128)S(1)} %get-tuple-element.17), channel_id=1, source_target_pairs={{0,1},{1,2},{2,3},{3,4},{4,5},{5,6},{6,7},{7,8},{8,9},{9,10},{10,1... | collective-permute-start | bytes 417800 | tf_op jit(solution)/shard_map/ppermute | solution.py:17
  122.0 14.7 %copy-start.7 = (bf16[512,256]{1,0:T(8,128)(2,1)S(1)}, bf16[512,256]{1,0:T(8,128)(2,1)}, u32[]{:S(2)}) copy-start(bf16[512,256]{1,0:T(8,128)(2,1)} %param.6) | copy-start | bytes 786436
  138.5 5.0 %copy-start.4 = (f32[1,16,8,128]{3,2,1,0:T(8,128)S(1)}, f32[1,16,8,128]{3,2,1,0:T(8,128)}, u32[]{:S(2)}) copy-start(f32[1,16,8,128]{3,2,1,0:T(8,128)} %get-tuple-element.57) | copy-start | bytes 196612
  139.9 14.4 %all-to-all-start.5 = ((bf16[16,2,8192]{2,1,0:T(2,128)(2,1)}), bf16[16,2,8192]{2,1,0:T(2,128)(2,1)S(1)}, u32[]{:S(2)}, u32[]{:S(2)}) async-start(bf16[16,2,8192]{2,1,0:T(2,128)(2,1)} %reshape.286), calls=%async_computation.5 | async-start | bytes 1048576 | tf_op jit(solution)/shard_map/all_to_all | solution.py:89
  156.1 8.8 %collective-permute-start.5 = (f32[17,16,1,128]{3,1,2,0:T(8,128)S(1)}, f32[17,16,1,128]{3,1,2,0:T(8,128)S(1)}, u32[]{:S(2)}, u32[]{:S(2)}) collective-permute-start(f32[17,16,1,128]{3,1,2,0:T(8,128)S(1)} %get-tuple-element.16), channel_id=1, source_target_pairs={{1,0},{2,1},{3,2},{4,3},{5,4},{6,5},{7,6},{8,7},{9,8},{10,9},{11,1... | collective-permute-start | bytes 417800 | tf_op jit(solution)/shard_map/ppermute | solution.py:19
  158.0 11.3 %collective-permute-start.4 = (f32[17,16,1,128]{3,1,2,0:T(8,128)S(1)}, f32[17,16,1,128]{3,1,2,0:T(8,128)S(1)}, u32[]{:S(2)}, u32[]{:S(2)}) collective-permute-start(f32[17,16,1,128]{3,1,2,0:T(8,128)S(1)} %get-tuple-element.15), channel_id=1, source_target_pairs={{0,1},{1,2},{2,3},{3,4},{4,5},{5,6},{6,7},{7,8},{8,9},{9,10},{10,1... | collective-permute-start | bytes 417800 | tf_op jit(solution)/shard_map/ppermute | solution.py:17
  170.8 15.9 %copy-start.8 = (bf16[512,256]{1,0:T(8,128)(2,1)S(1)}, bf16[512,256]{1,0:T(8,128)(2,1)}, u32[]{:S(2)}) copy-start(bf16[512,256]{1,0:T(8,128)(2,1)} %param.6) | copy-start | bytes 786436
  188.5 5.0 %copy-start.3 = (f32[1,16,8,128]{3,2,1,0:T(8,128)S(1)}, f32[1,16,8,128]{3,2,1,0:T(8,128)}, u32[]{:S(2)}) copy-start(f32[1,16,8,128]{3,2,1,0:T(8,128)} %get-tuple-element.58) | copy-start | bytes 196612
  189.9 14.4 %all-to-all-start.8 = ((bf16[16,2,8192]{2,1,0:T(2,128)(2,1)}), bf16[16,2,8192]{2,1,0:T(2,128)(2,1)S(1)}, u32[]{:S(2)}, u32[]{:S(2)}) async-start(bf16[16,2,8192]{2,1,0:T(2,128)(2,1)} %reshape.288), calls=%async_computation.8 | async-start | bytes 1048576 | tf_op jit(solution)/shard_map/all_to_all | solution.py:89
  206.1 8.0 %collective-permute-start.7 = (f32[17,16,1,128]{3,1,2,0:T(8,128)S(1)}, f32[17,16,1,128]{3,1,2,0:T(8,128)S(1)}, u32[]{:S(2)}, u32[]{:S(2)}) collective-permute-start(f32[17,16,1,128]{3,1,2,0:T(8,128)S(1)} %get-tuple-element.14), channel_id=1, source_target_pairs={{1,0},{2,1},{3,2},{4,3},{5,4},{6,5},{7,6},{8,7},{9,8},{10,9},{11,1... | collective-permute-start | bytes 417800 | tf_op jit(solution)/shard_map/ppermute | solution.py:19
  208.0 10.1 %collective-permute-start.6 = (f32[17,16,1,128]{3,1,2,0:T(8,128)S(1)}, f32[17,16,1,128]{3,1,2,0:T(8,128)S(1)}, u32[]{:S(2)}, u32[]{:S(2)}) collective-permute-start(f32[17,16,1,128]{3,1,2,0:T(8,128)S(1)} %get-tuple-element.13), channel_id=1, source_target_pairs={{0,1},{1,2},{2,3},{3,4},{4,5},{5,6},{6,7},{7,8},{8,9},{9,10},{10,1... | collective-permute-start | bytes 417800 | tf_op jit(solution)/shard_map/ppermute | solution.py:17
